TPU v7x, 32 devices: a whole 2x2x4 slice. The times are simulated.
32 devices in a mesh: dp: 8 (over y, x, core), tensor: 4 (over z).
Axes of the slice: x: 2, y: 2, z: 4, core: 2. Of those that a mesh axis runs over, the one named last changes fastest.
Arguments:
- hidden_in: bfloat16 [8192, 768], P(('dp', 'tensor')), may hold values from -40 to 40
- segment_ids: int32 [16, 512], P('dp'), may hold values from 0 to 7, never falling along the last dimension, each value on 1 to 256 neighbouring positions
- cotangent: float32 [8192, 768], P(('dp', 'tensor')), may hold values from -6 to 6
- norm1_gain: float32 [768], P(('dp', 'tensor')), may hold values from 0.5 to 1.5
- norm1_bias: float32 [768], P(('dp', 'tensor')), may hold values from -2 to 2
- norm2_gain: float32 [768], P(('dp', 'tensor')), may hold values from 0.5 to 1.5
- norm2_bias: float32 [768], P(('dp', 'tensor')), may hold values from -2 to 2
- qkv_weight: bfloat16 [768, 2304], P('dp', 'tensor'), may hold values from -2 to 2
- qkv_bias: bfloat16 [12, 192], P('tensor', 'dp'), may hold values from -3 to 3
- dense_weight: bfloat16 [768, 768], P('tensor', 'dp'), may hold values from -0.875 to 0.875
- dense_bias: float32 [768], P(('dp', 'tensor')), may hold values from -3 to 3
- up_weight: bfloat16 [768, 3072], P('dp', 'tensor'), may hold values from -0.21875 to 0.21875
- up_bias: bfloat16 [12, 256], P('tensor', 'dp'), may hold values from -3 to 3
- down_weight: bfloat16 [3072, 768], P('tensor', 'dp'), may hold values from -0.109375 to 0.109375
- down_bias: float32 [768], P(('dp', 'tensor')), may hold values from -3 to 3
Outputs:
- hidden_out: float32 [8192, 768], P(('dp', 'tensor'))
- hidden_grad: float32 [8192, 768], P(('dp', 'tensor'))
- norm1_gain_grad: float32 [768], P(('dp', 'tensor'))
- norm1_bias_grad: float32 [768], P(('dp', 'tensor'))
- norm2_gain_grad: float32 [768], P(('dp', 'tensor'))
- norm2_bias_grad: float32 [768], P(('dp', 'tensor'))
- qkv_weight_grad: float32 [768, 2304], P('dp', 'tensor')
- qkv_bias_grad: float32 [12, 192], P('tensor', 'dp')
- dense_weight_grad: float32 [768, 768], P('tensor', 'dp')
- dense_bias_grad: float32 [768], P(('dp', 'tensor'))
- up_weight_grad: float32 [768, 3072], P('dp', 'tensor')
- up_bias_grad: float32 [12, 256], P('tensor', 'dp')
- down_weight_grad: float32 [3072, 768], P('tensor', 'dp')
- down_bias_grad: float32 [768], P(('dp', 'tensor'))
Inputs may be any that keep to these rules, and one draw needn't show every extreme that they name: `segment_ids`: within each row of 512 tokens the ids never fall; each document holds 1 to 256 tokens, and some document holds exactly 256.
All inputs are finite; a program needn't handle non-finite values.
Results may differ from a plain program's by a relative error of at most 0.0082.
Values may be sent and summed in bfloat16 or wider, within the bound.
No kernel may reach another device: no remote copies, remote signals or barrier semaphores. Data moves between devices by JAX's collectives and lax.ppermute only.
A program may use at most 128 MiB of HBM per device.

v0:
```python
import math
import jax
import jax.numpy as jnp
from jax import lax
from jax.sharding import PartitionSpec as P

HD = 64
ROT = 16
BIAS_ROW = 256
norm_eps = 1e-05


def rotary_tables(length, rot_dims):
    places = jnp.arange(length).astype(jnp.float32)
    frequency = 1.0 / 10000.0 ** (jnp.arange(0, rot_dims, 2).astype(jnp.float32) / rot_dims)
    angles = places[:, None] * frequency[None, :]
    angles = jnp.concatenate([angles, angles], axis=1)
    return (jnp.cos(angles)[:, None, :], jnp.sin(angles)[:, None, :])


def rotate_apply(entries, cosine, sine, rot_dims):
    half_dims = rot_dims // 2
    front = entries[..., :rot_dims]
    turned = jnp.concatenate([-front[..., half_dims:], front[..., :half_dims]], axis=-1)
    return jnp.concatenate([front * cosine + turned * sine, entries[..., rot_dims:]], axis=-1)


def rotate_back(grads, cosine, sine, rot_dims):
    half_dims = rot_dims // 2
    front = grads[..., :rot_dims]
    scaled = front * sine
    turned = jnp.concatenate([scaled[..., half_dims:], -scaled[..., :half_dims]], axis=-1)
    return jnp.concatenate([front * cosine + turned, grads[..., rot_dims:]], axis=-1)


def normalize(wide_rows):
    centre = jnp.mean(wide_rows, axis=-1, keepdims=True)
    spread = jnp.mean(jnp.square(wide_rows - centre), axis=-1, keepdims=True)
    inverse = lax.rsqrt(spread + norm_eps)
    return ((wide_rows - centre) * inverse, inverse)


def gelu_exact(values):
    return 0.5 * values * (1.0 + lax.erf(values * (1.0 / math.sqrt(2.0))))


def gelu_slope(values):
    cumulative = 0.5 * (1.0 + lax.erf(values * (1.0 / math.sqrt(2.0))))
    density = jnp.exp(-0.5 * values * values) * (1.0 / math.sqrt(2.0 * math.pi))
    return cumulative + values * density


def allowed_pairs(segment):
    length = segment.shape[-1]
    earlier = lax.broadcasted_iota(jnp.int32, (length, length), 0) >= lax.broadcasted_iota(
        jnp.int32, (length, length), 1
    )
    return (segment[:, :, None] == segment[:, None, :]) & earlier[None]


def attend_scores(queries, key_rows, segment):
    scaling = queries.shape[-1] ** (-0.5)
    scores = (
        jnp.einsum("bqhd,bkhd->bhqk", queries, key_rows, preferred_element_type=jnp.float32)
        * scaling
    )
    return jnp.where(allowed_pairs(segment)[:, None], scores, -1e30)


def attend_forward(queries, key_rows, value_rows, segment):
    scores = attend_scores(queries, key_rows, segment)
    highest = jnp.max(scores, axis=-1, keepdims=True)
    logsum = highest + jnp.log(jnp.sum(jnp.exp(scores - highest), axis=-1, keepdims=True))
    weights = jnp.exp(scores - logsum).astype(jnp.bfloat16)
    output = jnp.einsum("bhqk,bkhd->bqhd", weights, value_rows, preferred_element_type=jnp.float32)
    return (output.astype(jnp.bfloat16), logsum)


def attend_backward(queries, key_rows, value_rows, segment, logsum, grad_out):
    scaling = queries.shape[-1] ** (-0.5)
    scores = attend_scores(queries, key_rows, segment)
    weights = jnp.exp(scores - logsum)
    weights_half = weights.astype(jnp.bfloat16)
    grad_weights = jnp.einsum(
        "bqhd,bkhd->bhqk", grad_out, value_rows, preferred_element_type=jnp.float32
    )
    inner_sum = jnp.sum(weights * grad_weights, axis=-1, keepdims=True)
    grad_scores = (weights * (grad_weights - inner_sum) * scaling).astype(jnp.bfloat16)
    grad_queries = jnp.einsum(
        "bhqk,bkhd->bqhd", grad_scores, key_rows, preferred_element_type=jnp.float32
    )
    grad_keys = jnp.einsum(
        "bhqk,bqhd->bkhd", grad_scores, queries, preferred_element_type=jnp.float32
    )
    grad_values = jnp.einsum(
        "bhqk,bqhd->bkhd", weights_half, grad_out, preferred_element_type=jnp.float32
    )
    return (grad_queries, grad_keys, grad_values)


def rows_product(left, right):
    return lax.dot_general(
        left, right, (((0,), (0,)), ((), ())), preferred_element_type=jnp.float32
    )


def cols_product(left, right):
    return lax.dot_general(
        left, right, (((1,), (1,)), ((), ())), preferred_element_type=jnp.float32
    )


def on_device(
    hidden_in,
    segment_ids,
    cotangent,
    norm1_gain,
    norm1_bias,
    norm2_gain,
    norm2_bias,
    qkv_weight,
    qkv_bias,
    dense_weight,
    dense_bias,
    up_weight,
    up_bias,
    down_weight,
    down_bias,
):
    gain_one, shift_one, gain_two, shift_two, dense_shift, down_shift = (
        lax.all_gather(norm1_gain, ("dp", "tensor"), axis=0, tiled=True),
        lax.all_gather(norm1_bias, ("dp", "tensor"), axis=0, tiled=True),
        lax.all_gather(norm2_gain, ("dp", "tensor"), axis=0, tiled=True),
        lax.all_gather(norm2_bias, ("dp", "tensor"), axis=0, tiled=True),
        lax.all_gather(dense_bias, ("dp", "tensor"), axis=0, tiled=True),
        lax.all_gather(down_bias, ("dp", "tensor"), axis=0, tiled=True),
    )
    qkv_full, up_full = (
        lax.all_gather(qkv_weight, "dp", axis=0, tiled=True),
        lax.all_gather(up_weight, "dp", axis=0, tiled=True),
    )
    dense_full, down_full, qkv_shift, up_shift = (
        lax.all_gather(dense_weight, "dp", axis=1, tiled=True),
        lax.all_gather(down_weight, "dp", axis=1, tiled=True),
        lax.all_gather(qkv_bias, "dp", axis=1, tiled=True),
        lax.all_gather(up_bias, "dp", axis=1, tiled=True),
    )
    seq_count = segment_ids.shape[0]
    length = segment_ids.shape[1]
    heads_here = qkv_full.shape[1] // (3 * HD)
    cosine, sine = rotary_tables(length, ROT)
    wide_rows = hidden_in.astype(jnp.float32)
    normed, inverse = normalize(wide_rows)
    first_local = (normed * gain_one + shift_one).astype(jnp.bfloat16)
    second_local = (normed * gain_two + shift_two).astype(jnp.bfloat16)
    first, second = (
        lax.all_gather(first_local, "tensor", axis=0, tiled=True),
        lax.all_gather(second_local, "tensor", axis=0, tiled=True),
    )
    mixed = jnp.dot(first, qkv_full, preferred_element_type=jnp.float32) + qkv_shift.reshape(
        -1
    ).astype(jnp.float32)
    mixed = mixed.reshape(seq_count, length, heads_here, 3, HD)
    queries = rotate_apply(mixed[..., 0, :], cosine, sine, ROT).astype(jnp.bfloat16)
    key_rows = rotate_apply(mixed[..., 1, :], cosine, sine, ROT).astype(jnp.bfloat16)
    value_rows = mixed[..., 2, :].astype(jnp.bfloat16)
    attended, logsum = attend_forward(queries, key_rows, value_rows, segment_ids)
    attended_flat = attended.reshape(seq_count * length, heads_here * HD)
    inner_pre = jnp.dot(second, up_full, preferred_element_type=jnp.float32) + up_shift.reshape(
        -1
    ).astype(jnp.float32)
    active = gelu_exact(inner_pre).astype(jnp.bfloat16)
    partial_value = jnp.dot(
        attended_flat, dense_full, preferred_element_type=jnp.float32
    ) + jnp.dot(active, down_full, preferred_element_type=jnp.float32)
    branch = lax.psum_scatter(partial_value, "tensor", scatter_dimension=0, tiled=True)
    hidden_out = wide_rows + branch + dense_shift + down_shift
    qkv_back, up_back = (
        lax.all_gather(qkv_weight, "dp", axis=0, tiled=True),
        lax.all_gather(up_weight, "dp", axis=0, tiled=True),
    )
    dense_back, down_back = (
        lax.all_gather(dense_weight, "dp", axis=1, tiled=True),
        lax.all_gather(down_weight, "dp", axis=1, tiled=True),
    )
    cotangent_all = lax.all_gather(cotangent.astype(jnp.bfloat16), "tensor", axis=0, tiled=True)
    grad_down = rows_product(active, cotangent_all)
    grad_active = cols_product(cotangent_all, down_back)
    grad_pre = grad_active * gelu_slope(inner_pre)
    grad_pre_half = grad_pre.astype(jnp.bfloat16)
    grad_up = rows_product(second, grad_pre_half)
    second_part = cols_product(grad_pre_half, up_back)
    grad_dense = rows_product(attended_flat, cotangent_all)
    grad_attended = (
        cols_product(cotangent_all, dense_back)
        .astype(jnp.bfloat16)
        .reshape(seq_count, length, heads_here, HD)
    )
    grad_queries, grad_keys, grad_values = attend_backward(
        queries, key_rows, value_rows, segment_ids, logsum, grad_attended
    )
    grad_mixed = jnp.stack(
        [
            rotate_back(grad_queries, cosine, sine, ROT),
            rotate_back(grad_keys, cosine, sine, ROT),
            grad_values,
        ],
        axis=3,
    )
    grad_mixed = grad_mixed.reshape(seq_count * length, heads_here * 3 * HD)
    grad_mixed_half = grad_mixed.astype(jnp.bfloat16)
    grad_qkv = rows_product(first, grad_mixed_half)
    first_part = cols_product(grad_mixed_half, qkv_back)
    grad_first, grad_second = (
        lax.psum_scatter(first_part, "tensor", scatter_dimension=0, tiled=True),
        lax.psum_scatter(second_part, "tensor", scatter_dimension=0, tiled=True),
    )
    grad_normed = grad_first * gain_one + grad_second * gain_two
    stat_terms = (
        jnp.sum(grad_first * normed, axis=0),
        jnp.sum(grad_first, axis=0),
        jnp.sum(grad_second * normed, axis=0),
        jnp.sum(grad_second, axis=0),
    )
    grad_rows = inverse * (
        grad_normed
        - jnp.mean(grad_normed, axis=-1, keepdims=True)
        - normed * jnp.mean(grad_normed * normed, axis=-1, keepdims=True)
    )
    hidden_grad = cotangent + grad_rows
    gain_one_grad, shift_one_grad, gain_two_grad, shift_two_grad, shift_out_grad = (
        lax.psum_scatter(stat_terms[0], ("dp", "tensor"), scatter_dimension=0, tiled=True),
        lax.psum_scatter(stat_terms[1], ("dp", "tensor"), scatter_dimension=0, tiled=True),
        lax.psum_scatter(stat_terms[2], ("dp", "tensor"), scatter_dimension=0, tiled=True),
        lax.psum_scatter(stat_terms[3], ("dp", "tensor"), scatter_dimension=0, tiled=True),
        lax.psum_scatter(
            jnp.sum(cotangent, axis=0), ("dp", "tensor"), scatter_dimension=0, tiled=True
        ),
    )
    qkv_grad, up_grad = (
        lax.psum_scatter(grad_qkv, "dp", scatter_dimension=0, tiled=True),
        lax.psum_scatter(grad_up, "dp", scatter_dimension=0, tiled=True),
    )
    dense_grad, down_grad, qkv_bias_grad, up_bias_grad = (
        lax.psum_scatter(grad_dense, "dp", scatter_dimension=1, tiled=True),
        lax.psum_scatter(grad_down, "dp", scatter_dimension=1, tiled=True),
        lax.psum_scatter(
            jnp.sum(grad_mixed, axis=0).reshape(heads_here, 3 * HD),
            "dp",
            scatter_dimension=1,
            tiled=True,
        ),
        lax.psum_scatter(
            jnp.sum(grad_pre, axis=0).reshape(-1, BIAS_ROW), "dp", scatter_dimension=1, tiled=True
        ),
    )
    return (
        hidden_out,
        hidden_grad,
        gain_one_grad,
        shift_one_grad,
        gain_two_grad,
        shift_two_grad,
        qkv_grad,
        qkv_bias_grad,
        dense_grad,
        shift_out_grad,
        up_grad,
        up_bias_grad,
        down_grad,
        shift_out_grad,
    )


def solution(mesh):
    return jax.shard_map(
        on_device,
        mesh=mesh,
        in_specs=(
            P(("dp", "tensor"), None),
            P("dp", None),
            P(("dp", "tensor"), None),
            P(("dp", "tensor")),
            P(("dp", "tensor")),
            P(("dp", "tensor")),
            P(("dp", "tensor")),
            P("dp", "tensor"),
            P("tensor", "dp"),
            P("tensor", "dp"),
            P(("dp", "tensor")),
            P("dp", "tensor"),
            P("tensor", "dp"),
            P("tensor", "dp"),
            P(("dp", "tensor")),
        ),
        out_specs=(
            P(("dp", "tensor"), None),
            P(("dp", "tensor"), None),
            P(("dp", "tensor")),
            P(("dp", "tensor")),
            P(("dp", "tensor")),
            P(("dp", "tensor")),
            P("dp", "tensor"),
            P("tensor", "dp"),
            P("tensor", "dp"),
            P(("dp", "tensor")),
            P("dp", "tensor"),
            P("tensor", "dp"),
            P("tensor", "dp"),
            P(("dp", "tensor")),
        ),
        check_vma=False,
    )
```

profile of v0, /device:TPU:0, one launch (start us, length us, event | category | flops | bytes accessed | tf_op | source)
XLA Modules:
  0.0 633.8 jit_solution(11862884323727938177)
XLA Ops:
  7.3 1.1 convert_reduce_fusion
  8.4 1.2 fusion.57
  9.7 0.9 dynamic-update-slice
  10.6 0.8 dynamic-update-slice.1
  12.2 0.8 dynamic-update-slice.3
  13.1 42.2 %all-reduce.13 = (f32[768]{0:T(1024)S(1)}, f32[768]{0:T(1024)S(1)}, f32[768]{0:T(1024)S(1)}, f32[768]{0:T(1024)S(1)}) all-reduce(f32[768]{0:T(1024)S(1)} %dynamic-update-slice.3, f32[768]{0:T(1024)S(1)} %dynamic-update-slice.2, f32[768]{0:T(1024)S(1)} %dynamic-update-slice.1, ...), channel_id=1, replica_groups=mesh['dp'=8,'tensor'=4] {'dp','tensor'}, use_global_device_ids=true, to_apply=%add.3 | all-reduce | flops 3072 | bytes 24576
  55.3 2.2 fusion.48
  57.5 1.9 convert_element_type.98
  61.6 11.6 %all_gather.52 = bf16[768,576]{1,0:T(8,128)(2,1)S(1)} all-gather(bf16[96,576]{1,0:T(8,128)(2,1)S(1)} %copy-done.18), channel_id=1, replica_groups=mesh['dp'=8,'tensor'=4] {'dp'}, dimensions={0}, use_global_device_ids=true | all-gather | bytes 995328 | tf_op jit(solution)/shard_map/all_gather | solution.py:139
  73.2 7.9 %all-gather = bf16[8,24,3]{1,2,0:T(4,128)(2,1)S(1)} all-gather(bf16[1,24,3]{1,2,0:T(4,128)(2,1)S(1)} %bitcast.91), channel_id=1, replica_groups=mesh['dp'=8,'tensor'=4] {'dp'}, dimensions={0}, use_global_device_ids=true | all-gather | bytes 1296 | tf_op jit(solution)/shard_map/all_gather | solution.py:145
  81.5 9.6 %all_gather.54 = bf16[192,768]{0,1:T(8,128)(2,1)S(1)} all-gather(bf16[192,96]{0,1:T(8,128)(2,1)S(1)} %copy.86), channel_id=1, replica_groups=mesh['dp'=8,'tensor'=4] {'dp'}, dimensions={1}, use_global_device_ids=true | all-gather | bytes 331776 | tf_op jit(solution)/shard_map/all_gather | solution.py:143
  91.1 7.9 %all-gather.1 = bf16[8,32,3]{1,2,0:T(4,128)(2,1)S(1)} all-gather(bf16[1,32,3]{1,2,0:T(4,128)(2,1)S(1)} %bitcast.92), channel_id=1, replica_groups=mesh['dp'=8,'tensor'=4] {'dp'}, dimensions={0}, use_global_device_ids=true | all-gather | bytes 1728 | tf_op jit(solution)/shard_map/all_gather | solution.py:146
  100.2 4.1 convolution_add_fusion.1
  104.4 3.8 reshape.175
  109.2 1.0 slice.83
  110.3 1.3 fusion.2
  111.7 1.4 exponential_reduce_fusion
  113.1 1.2 copy-done.1
  114.3 18.3 %all-gather.16.cloned.1.call-done = bf16[1024,768]{1,0:T(8,128)(2,1)} async-done(((bf16[256,768]{1,0:T(8,128)(2,1)}), bf16[1024,768]{1,0:T(8,128)(2,1)}) %all-gather.16.cloned.1.call-update) | async-done | bytes 1572880 | tf_op jit(solution)/shard_map/all_gather | solution.py:186
  132.6 2.1 convolution_convert_fusion
  135.0 3.7 fusion.66
  138.7 12.8 %fusion.27 = f32[2,512,3,64]{1,3,2,0:T(8,128)S(1)} fusion(f32[2,3,512,512]{2,3,1,0:T(8,128)} %fusion.66, bf16[2,512,3,48]{1,3,2,0:T(8,128)(2,1)S(1)} %copy-done.16, bf16[2,512,3,16]{1,3,2,0:T(8,128)(2,1)S(1)} %get-tuple-element.51, f32[2,3,512,512]{2,3,1,0:T(8,128)} %copy-done.1, f32[2,3,512]{2,1,0:T(4,128)S(1)} %log_add_fusion, ...), kind=kOutput, calls=%fused_computation.31 | convolution fusion | flops 219418112 | bytes 14299136 | tf_op jit(solution)/shard_map/bhqk,bkhd->bqhd/dot_general | solution.py:89
  151.5 0.9 slice.97
  152.4 13.1 %fusion.30 = f32[2,512,3,64]{1,3,2,0:T(8,128)S(1)} fusion(f32[2,3,512,512]{2,3,1,0:T(8,128)} %fusion.66, bf16[2,512,3,48]{1,3,2,0:T(8,128)(2,1)} %copy-done.17, bf16[2,512,3,16]{1,3,2,0:T(8,128)(2,1)S(1)} %get-tuple-element.50, f32[2,3,512,512]{2,3,1,0:T(8,128)} %copy-done.1, f32[2,3,512]{2,1,0:T(4,128)S(1)} %log_add_fusion, ...), kind=kOutput, calls=%fused_computation.32 | convolution fusion | flops 219418112 | bytes 14299136 | tf_op jit(solution)/shard_map/bhqk,bqhd->bkhd/dot_general | solution.py:92
  165.5 0.9 slice.101
  166.4 4.6 fusion.36
  171.7 24.1 %all-gather.10.cloned.1.call-done = bf16[1024,768]{1,0:T(8,128)(2,1)} async-done(((bf16[256,768]{1,0:T(8,128)(2,1)}), bf16[1024,768]{1,0:T(8,128)(2,1)}) %all-gather.10.cloned.1.call-update) | async-done | bytes 1572880 | tf_op jit(solution)/shard_map/all_gather | solution.py:158
  195.7 5.4 multiply_convert_fusion.1
  201.2 19.1 %all-gather.14.cloned.1.call-done = bf16[768,768]{0,1:T(8,128)(2,1)} async-done(((bf16[768,96]{0,1:T(8,128)(2,1)}), bf16[768,768]{0,1:T(8,128)(2,1)}) %all-gather.14.cloned.1.call-update) | async-done | bytes 1179664 | tf_op jit(solution)/shard_map/all_gather | solution.py:144
  220.3 5.6 fusion.90
  225.9 1.3 reshape.179
  227.2 1.5 copy.103
  228.7 1.7 maximum_add_fusion
  230.4 1.1 maximum_bitcast_fusion
  231.5 1.6 convolution_bitcast_fusion
  233.2 1.2 maximum_bitcast_fusion.1
  234.4 4.8 fusion.24
  239.5 1.2 copy.93
  241.0 1.0 copy-done.11
  242.0 3.2 fusion.92
  245.3 4.8 fusion.62
  250.4 3.2 fusion.91
  253.6 2.3 convolution_add_fusion
  256.0 4.5 fusion.93
  260.6 4.8 fusion.60
  265.4 4.3 fusion.94
  269.7 1.3 dynamic-slice.4
  271.7 0.9 dynamic-update-slice.4
  272.6 0.8 dynamic-update-slice.5
  273.4 1.3 fusion.18
  274.9 13.1 %all-reduce.10 = f32[3,192]{1,0:T(4,128)S(1)} all-reduce(f32[3,192]{1,0:T(4,128)S(1)} %reshape.178), channel_id=10, replica_groups=mesh['dp'=8,'tensor'=4] {'dp'}, use_global_device_ids=true, to_apply=%region_20.21.clone | all-reduce | flops 576 | bytes 4608
  288.6 1.4 copy.104
  289.9 11.2 %reduce-scatter.26.cloned.1.call-done = f32[96,192]{1,0:T(8,128)} async-done(((f32[768,192]{1,0:T(8,128)}), f32[96,192]{1,0:T(8,128)}) %reduce-scatter.26.cloned.1.call-update) | async-done | bytes 73744
  301.1 1.6 copy.102
  302.8 61.1 %reduce-scatter.16.cloned.1.call-done = f32[256,768]{1,0:T(8,128)} async-done(((f32[1024,768]{1,0:T(8,128)}), f32[256,768]{1,0:T(8,128)}) %reduce-scatter.16.cloned.1.call-update) | async-done | bytes 786448 | tf_op jit(solution)/shard_map/reduce_scatter | solution.py:215
  363.9 62.7 %reduce-scatter.18.cloned.1.call-done = f32[256,768]{1,0:T(8,128)} async-done(((f32[1024,768]{1,0:T(8,128)}), f32[256,768]{1,0:T(8,128)}) %reduce-scatter.18.cloned.1.call-update) | async-done | bytes 786448 | tf_op jit(solution)/shard_map/reduce_scatter | solution.py:216
  426.5 1.9 fusion.86
  428.5 1.2 fusion.54
  429.6 43.5 %all-reduce.12 = (f32[768]{0:T(1024)S(1)}, f32[768]{0:T(1024)S(1)}, f32[768]{0:T(1024)S(1)}, f32[768]{0:T(1024)S(1)}, f32[768]{0:T(1024)S(1)}, /*index=5*/f32[768]{0:T(1024)S(1)}, f32[768]{0:T(1024)S(1)}) all-reduce(f32[768]{0:T(1024)S(1)} %dynamic-update-slice.5, ...), channel_id=1, replica_groups=mesh['dp'=8,'tensor'=4] {'dp','tensor'}, use_global_device_ids=true, to_apply=%add.5 | all-reduce | flops 5376 | bytes 43008
  475.5 14.4 %reduce-scatter.14.cloned.1.call-done = f32[256,768]{1,0:T(8,128)} async-done(((f32[1024,768]{1,0:T(8,128)}), f32[256,768]{1,0:T(8,128)}) %reduce-scatter.14.cloned.1.call-update) | async-done | bytes 786448 | tf_op jit(solution)/shard_map/reduce_scatter | solution.py:176
  489.9 2.1 fusion.59
  492.0 42.1 %reduce-scatter.20.cloned.1.call-done = f32[96,576]{1,0:T(8,128)} async-done(((f32[768,576]{1,0:T(8,128)}), f32[96,576]{1,0:T(8,128)}) %reduce-scatter.20.cloned.1.call-update) | async-done | bytes 221200 | tf_op jit(solution)/shard_map/reduce_scatter | solution.py:241
  534.1 46.1 %reduce-scatter.22.cloned.1.call-done = f32[96,768]{1,0:T(8,128)} async-done(((f32[768,768]{1,0:T(8,128)}), f32[96,768]{1,0:T(8,128)}) %reduce-scatter.22.cloned.1.call-update) | async-done | bytes 294928 | tf_op jit(solution)/shard_map/reduce_scatter | solution.py:242
  580.3 46.3 %reduce-scatter.24.cloned.1.call-done = f32[768,96]{0,1:T(8,128)} async-done(((f32[768,768]{0,1:T(8,128)}), f32[768,96]{0,1:T(8,128)}) %reduce-scatter.24.cloned.1.call-update) | async-done | bytes 294928 | tf_op jit(solution)/shard_map/reduce_scatter | solution.py:246
  (126 shorter events, 11.3 us)
Async XLA Ops:
  7.2 54.4 %copy-start.18 = (bf16[96,576]{1,0:T(8,128)(2,1)S(1)}, bf16[96,576]{1,0:T(8,128)(2,1)}, u32[]{:S(2)}) copy-start(bf16[96,576]{1,0:T(8,128)(2,1)} %param.22) | copy-start | bytes 331780
  7.2 66.0 %copy-start.22 = (bf16[3,24]{1,0:T(4,128)(2,1)S(1)}, bf16[3,24]{1,0:T(4,128)(2,1)}, u32[]{:S(2)}) copy-start(bf16[3,24]{1,0:T(4,128)(2,1)} %param.23) | copy-start | bytes 436
  7.2 74.2 %copy-start.19 = (bf16[192,96]{1,0:T(8,128)(2,1)S(1)}, bf16[192,96]{1,0:T(8,128)(2,1)}, u32[]{:S(2)}) copy-start(bf16[192,96]{1,0:T(8,128)(2,1)} %param.24) | copy-start | bytes 110596
  7.2 93.0 %all-gather.8.cloned.1.call-start = ((), (), s32[]{:S(2)}) async-start(), calls=%async_computation.8 | async-start | bytes 1966080 | tf_op jit(solution)/shard_map/all_gather | solution.py:157
  8.4 82.7 %copy-start.23 = (bf16[3,32]{1,0:T(4,128)(2,1)S(1)}, bf16[3,32]{1,0:T(4,128)(2,1)}, u32[]{:S(2)}) copy-start(bf16[3,32]{1,0:T(4,128)(2,1)} %param.27) | copy-start | bytes 580
  8.4 91.3 %copy-start.20 = (s32[2,512]{1,0:T(2,128)S(1)}, s32[2,512]{1,0:T(2,128)}, u32[]{:S(2)}) copy-start(s32[2,512]{1,0:T(2,128)} %param.16) | copy-start | bytes 12292
  57.5 75.1 %all-gather.16.cloned.1.call-start = ((), (), s32[]{:S(2)}) async-start(), calls=%async_computation.13 | async-start | bytes 1966080 | tf_op jit(solution)/shard_map/all_gather | solution.py:186
  59.5 112.2 %all-gather.12.cloned.1.call-start = ((), (), s32[]{:S(2)}) async-start(), calls=%async_computation.10 | async-start | bytes 1327104 | tf_op jit(solution)/shard_map/all_gather | solution.py:140
  60.2 135.5 %all-gather.10.cloned.1.call-start = ((), (), s32[]{:S(2)}) async-start(), calls=%async_computation.9 | async-start | bytes 1966080 | tf_op jit(solution)/shard_map/all_gather | solution.py:158
  60.8 159.5 %all-gather.14.cloned.1.call-start = ((), (), s32[]{:S(2)}) async-start(), calls=%async_computation.11 | async-start | bytes 1327104 | tf_op jit(solution)/shard_map/all_gather | solution.py:144
  61.4 227.2 %reduce-scatter.28.cloned.1.call-start = ((), (), s32[]{:S(2)}) async-start(), calls=%async_computation.20 | async-start | bytes 147456
  73.2 27.1 %copy-start.12 = (bf16[768,576]{1,0:T(8,128)(2,1)}, bf16[768,576]{1,0:T(8,128)(2,1)S(1)}, u32[]{:S(2)}) copy-start(bf16[768,576]{1,0:T(8,128)(2,1)S(1)} %all_gather.52) | copy-start | bytes 2654212
  81.4 28.8 %copy-start.14 = (f32[512,16]{0,1:T(8,128)}, f32[512,16]{0,1:T(8,128)S(1)}, u32[]{:S(2)}) copy-start(f32[512,16]{0,1:T(8,128)S(1)} %get-tuple-element.56) | copy-start | bytes 98308
  100.2 66.2 %copy-start.7 = (pred[2,512,512]{1,2,0:T(8,128)(4,1)}, pred[2,512,512]{1,2,0:T(8,128)(4,1)S(1)}, u32[]{:S(2)}) copy-start(pred[2,512,512]{1,2,0:T(8,128)(4,1)S(1)} %compare_and_fusion) | copy-start | bytes 1572868
  109.1 2.6 copy-start.15
  109.2 2.5 copy-start.17
  111.7 2.6 copy-start.1
  114.3 20.7 %copy-start.9 = (bf16[2,512,3,1,64]{1,0,4,3,2:T(2,128)(2,1)S(1)}, bf16[2,512,3,1,64]{1,0,4,3,2:T(2,128)(2,1)}, u32[]{:S(2)}) copy-start(bf16[2,512,3,1,64]{1,0,4,3,2:T(2,128)(2,1)} %slice.83) | copy-start | bytes 1179652
  114.3 52.1 %copy-start.21 = (f32[2,3,512]{2,1,0:T(4,128)}, f32[2,3,512]{2,1,0:T(4,128)S(1)}, u32[]{:S(2)}) copy-start(f32[2,3,512]{2,1,0:T(4,128)S(1)} %log_add_fusion) | copy-start | bytes 36868
  134.9 3.7 copy-start.8
  134.9 3.7 copy-start.16
  165.5 6.0 copy-start.10
  171.5 60.0 %copy-start.3 = (bf16[24,8,2,512]{3,1,2,0:T(8,128)(2,1)}, bf16[24,8,2,512]{3,1,2,0:T(8,128)(2,1)S(1)}, u32[]{:S(2)}) copy-start(bf16[24,8,2,512]{3,1,2,0:T(8,128)(2,1)S(1)} %copy.108) | copy-start | bytes 1179652
  171.6 48.7 %copy-start.2 = (bf16[1024,768]{1,0:T(8,128)(2,1)S(1)}, bf16[1024,768]{1,0:T(8,128)(2,1)}, u32[]{:S(2)}) copy-start(bf16[1024,768]{1,0:T(8,128)(2,1)} %all-gather.16.cloned.1.call-done) | copy-start | bytes 4718596
  228.7 72.5 %reduce-scatter.26.cloned.1.call-start = ((), (), s32[]{:S(2)}) async-start(), calls=%async_computation.19 | async-start | bytes 884736
  234.3 129.5 %reduce-scatter.16.cloned.1.call-start = ((), (), s32[]{:S(2)}) async-start(), calls=%async_computation.14 | async-start | bytes 3932160 | tf_op jit(solution)/shard_map/reduce_scatter | solution.py:215
  239.2 1.8 copy-start.5
  239.5 2.6 copy-start.13
  241.0 1.0 copy-start.11
  245.3 181.3 %reduce-scatter.18.cloned.1.call-start = ((), (), s32[]{:S(2)}) async-start(), calls=%async_computation.15 | async-start | bytes 3932160 | tf_op jit(solution)/shard_map/reduce_scatter | solution.py:216
  250.1 239.8 %reduce-scatter.14.cloned.1.call-start = ((), (), s32[]{:S(2)}) async-start(), calls=%async_computation.12 | async-start | bytes 3932160 | tf_op jit(solution)/shard_map/reduce_scatter | solution.py:176
  250.4 3.2 copy-start.4
  256.0 278.2 %reduce-scatter.20.cloned.1.call-start = ((), (), s32[]{:S(2)}) async-start(), calls=%async_computation.16 | async-start | bytes 2211840 | tf_op jit(solution)/shard_map/reduce_scatter | solution.py:241
  260.5 319.7 %reduce-scatter.22.cloned.1.call-start = ((), (), s32[]{:S(2)}) async-start(), calls=%async_computation.17 | async-start | bytes 2654208 | tf_op jit(solution)/shard_map/reduce_scatter | solution.py:242
  265.4 361.2 %reduce-scatter.24.cloned.1.call-start = ((), (), s32[]{:S(2)}) async-start(), calls=%async_computation.18 | async-start | bytes 2654208 | tf_op jit(solution)/shard_map/reduce_scatter | solution.py:246
  269.7 156.8 %copy-start = (bf16[256,768]{1,0:T(8,128)(2,1)S(1)}, bf16[256,768]{1,0:T(8,128)(2,1)}, u32[]{:S(2)}) copy-start(bf16[256,768]{1,0:T(8,128)(2,1)} %param.15) | copy-start | bytes 1179652
  269.7 158.7 %copy-start.6 = (f32[256,768]{1,0:T(8,128)S(1)}, f32[256,768]{1,0:T(8,128)}, u32[]{:S(2)}) copy-start(f32[256,768]{1,0:T(8,128)} %param.17) | copy-start | bytes 2359300
  473.2 153.9 %copy-start.24 = (f32[24]{0:T(128)}, f32[24]{0:T(128)S(1)}, u32[]{:S(2)}) copy-start(f32[24]{0:T(128)S(1)} %dynamic-slice.6) | copy-start | bytes 292
Sparse Core Ops, SparseCore 0:
  57.6 36.8 all-gather.7
  96.6 35.8 all-gather.15
  134.4 22.7 all-gather.11
  158.7 37.0 all-gather.9
  197.5 22.7 all-gather.13
  228.8 33.5 reduce-scatter.27
  266.1 34.9 reduce-scatter.25
  303.4 60.3 reduce-scatter.15
  366.2 60.3 reduce-scatter.17
  428.7 61.1 reduce-scatter.13
  493.9 40.1 reduce-scatter.19
  537.9 42.3 reduce-scatter.21
  584.2 42.3 reduce-scatter.23
where the time goes:
time: 640 us; the launch traced here: 634 us
  waiting for transfers between devices  347 us (54%)
  blocking collectives  136 us (21%)
  matrix products  86.3 us (13%)
  local copies, waits for them, and re-layouts  28.8 us (4%)
  other arithmetic  19.6 us (3%)
  between operations  15.4 us (2%)
    unnamed x3, blocking collectives  98.7 us
    reduce_scatter x1, waiting for transfers between devices, on_device(): lax.psum_scatter(second_part, 'tensor', scatter_dimension=0, tiled=True)  62.7 us
    reduce_scatter x1, waiting for transfers between devices, on_device(): lax.psum_scatter(first_part, 'tensor', scatter_dimension=0, tiled=True)  61.1 us
    reduce_scatter x1, waiting for transfers between devices, on_device(): lax.psum_scatter(grad_down, 'dp', scatter_dimension=1, tiled=True)  46.3 us
    reduce_scatter x1, waiting for transfers between devices, on_device(): lax.psum_scatter(grad_up, 'dp', scatter_dimension=0, tiled=True)  46.1 us
    reduce_scatter x1, waiting for transfers between devices, on_device(): lax.psum_scatter(grad_qkv, 'dp', scatter_dimension=0, tiled=True)  42.1 us
    all_gather x1, waiting for transfers between devices, on_device(): lax.all_gather(second_local, 'tensor', axis=0, tiled=True)  24.1 us
    all_gather x1, waiting for transfers between devices, on_device(): lax.all_gather(down_weight, 'dp', axis=1, tiled=True)  19.1 us
  transfers between devices with their start and end apart: 13, of which 10 were waited for; matrix products, arithmetic and copies ran while one was open for 18% of the time, Pallas kernels for 0%

commit v1 on v0

--- a/solution.py
+++ b/solution.py
@@ -155,7 +155,10 @@
     second_local = (normed * gain_two + shift_two).astype(jnp.bfloat16)
     first, second = (
         lax.all_gather(first_local, "tensor", axis=0, tiled=True),
-        lax.all_gather(second_local, "tensor", axis=0, tiled=True),
+        jnp.concatenate(
+            lax.all_to_all(jnp.stack([second_local] * lax.axis_size("tensor")), "tensor", 0, 0),
+            axis=0,
+        ),
     )
     mixed = jnp.dot(first, qkv_full, preferred_element_type=jnp.float32) + qkv_shift.reshape(
         -1

time: 640 us -> 631 us (0.986)
  waiting for transfers between devices: 347 us -> 326 us
    all_gather x1 -> x0, waiting for transfers between devices: 24.1 us -> none  [on_device(): lax.all_gather(second_local, 'tensor', axis=0, tiled=True)]
    all_gather x1, waiting for transfers between devices: 19.1 us -> 0.01 us  [on_device(): lax.all_gather(down_weight, 'dp', axis=1, tiled=True)]
    all_gather x1, waiting for transfers between devices: 0.02 us -> 17 us  [on_device(): lax.all_gather(first_local, 'tensor', axis=0, tiled=True)]
    all_gather x1, waiting for transfers between devices: 18.3 us -> 24.7 us  [on_device(): lax.all_gather(cotangent.astype(jnp.bfloat16), 'tensor', axis=0, tiled=True)]
    unnamed x15 -> x14, waiting for transfers between devices: 13.1 us -> 11.6 us
    unnamed x76 -> x96, local copies, waits for them, and re-layouts: 17.1 us -> 17.2 us
  transfers between devices with their start and end apart: 13 -> 13, of which waited for: 10 -> 9; matrix products, arithmetic and copies ran while one was open for 18% -> 20% of each run, Pallas kernels for 0% -> 0%
where the time goes in v1:
time: 631 us; the launch traced here: 625 us
  waiting for transfers between devices  326 us (52%)
  blocking collectives  136 us (22%)
  matrix products  86.7 us (14%)
  local copies, waits for them, and re-layouts  31.5 us (5%)
  other arithmetic  24.3 us (4%)
  between operations  15.7 us (2%)
    unnamed x3, blocking collectives  98.6 us
    reduce_scatter x1, waiting for transfers between devices, on_device(): lax.psum_scatter(second_part, 'tensor', scatter_dimension=0, tiled=True)  62.6 us
    reduce_scatter x1, waiting for transfers between devices, on_device(): lax.psum_scatter(first_part, 'tensor', scatter_dimension=0, tiled=True)  61.1 us
    reduce_scatter x1, waiting for transfers between devices, on_device(): lax.psum_scatter(grad_up, 'dp', scatter_dimension=0, tiled=True)  46.3 us
    reduce_scatter x1, waiting for transfers between devices, on_device(): lax.psum_scatter(grad_down, 'dp', scatter_dimension=1, tiled=True)  46.2 us
    reduce_scatter x1, waiting for transfers between devices, on_device(): lax.psum_scatter(grad_qkv, 'dp', scatter_dimension=0, tiled=True)  41.9 us
    all_gather x1, waiting for transfers between devices, on_device(): lax.all_gather(cotangent.astype(jnp.bfloat16), 'tensor', axis=0, tiled=True)  24.7 us
    unnamed x96, local copies, waits for them, and re-layouts  17.2 us
  transfers between devices with their start and end apart: 13, of which 9 were waited for; matrix products, arithmetic and copies ran while one was open for 20% of the time, Pallas kernels for 0%

profile of v1, /device:TPU:0, one launch (start us, length us, event | category | flops | bytes accessed | tf_op | source)
XLA Modules:
  0.0 625.2 jit_solution(15156456520382054339)
XLA Ops:
  7.2 1.1 convert_reduce_fusion
  8.4 1.2 fusion.57
  9.6 0.9 dynamic-update-slice
  13.0 42.2 %all-reduce.13 = (f32[768]{0:T(1024)S(1)}, f32[768]{0:T(1024)S(1)}, f32[768]{0:T(1024)S(1)}, f32[768]{0:T(1024)S(1)}) all-reduce(f32[768]{0:T(1024)S(1)} %dynamic-update-slice.3, f32[768]{0:T(1024)S(1)} %dynamic-update-slice.2, f32[768]{0:T(1024)S(1)} %dynamic-update-slice.1, ...), channel_id=1, replica_groups=mesh['dp'=8,'tensor'=4] {'dp','tensor'}, use_global_device_ids=true, to_apply=%add.3 | all-reduce | flops 3072 | bytes 24576
  55.2 2.0 fusion.48
  57.3 1.9 convert_element_type.98
  60.0 1.3 stack.19
  61.3 4.5 all-to-all-start
  66.5 11.6 %all_gather.49 = bf16[768,576]{1,0:T(8,128)(2,1)S(1)} all-gather(bf16[96,576]{1,0:T(8,128)(2,1)S(1)} %copy-done.24), channel_id=1, replica_groups=mesh['dp'=8,'tensor'=4] {'dp'}, dimensions={0}, use_global_device_ids=true | all-gather | bytes 995328 | tf_op jit(solution)/shard_map/all_gather | solution.py:139
  78.1 8.1 %all-gather = bf16[8,24,3]{1,2,0:T(4,128)(2,1)S(1)} all-gather(bf16[1,24,3]{1,2,0:T(4,128)(2,1)S(1)} %bitcast.92), channel_id=1, replica_groups=mesh['dp'=8,'tensor'=4] {'dp'}, dimensions={0}, use_global_device_ids=true | all-gather | bytes 1296 | tf_op jit(solution)/shard_map/all_gather | solution.py:145
  87.2 9.4 %all_gather.51 = bf16[192,768]{0,1:T(8,128)(2,1)S(1)} all-gather(bf16[192,96]{0,1:T(8,128)(2,1)S(1)} %copy.86), channel_id=1, replica_groups=mesh['dp'=8,'tensor'=4] {'dp'}, dimensions={1}, use_global_device_ids=true | all-gather | bytes 331776 | tf_op jit(solution)/shard_map/all_gather | solution.py:143
  96.7 8.1 %all-gather.1 = bf16[8,32,3]{1,2,0:T(4,128)(2,1)S(1)} all-gather(bf16[1,32,3]{1,2,0:T(4,128)(2,1)S(1)} %bitcast.93), channel_id=1, replica_groups=mesh['dp'=8,'tensor'=4] {'dp'}, dimensions={0}, use_global_device_ids=true | all-gather | bytes 1728 | tf_op jit(solution)/shard_map/all_gather | solution.py:146
  105.4 1.2 compare_and_fusion
  106.7 17.0 %all-gather.7.cloned.1.call-done = bf16[1024,768]{1,0:T(8,128)(2,1)} async-done(((bf16[256,768]{1,0:T(8,128)(2,1)}), bf16[1024,768]{1,0:T(8,128)(2,1)}) %all-gather.7.cloned.1.call-update) | async-done | bytes 1572880 | tf_op jit(solution)/shard_map/all_gather | solution.py:157
  123.7 4.0 convolution_add_fusion.1
  127.7 3.8 reshape.180
  135.3 1.0 slice.83
  136.4 24.7 %all-gather.13.cloned.1.call-done = bf16[1024,768]{1,0:T(8,128)(2,1)} async-done(((bf16[256,768]{1,0:T(8,128)(2,1)}), bf16[1024,768]{1,0:T(8,128)(2,1)}) %all-gather.13.cloned.1.call-update) | async-done | bytes 1572880 | tf_op jit(solution)/shard_map/all_gather | solution.py:189
  161.0 2.1 convolution_convert_fusion
  163.5 1.1 fusion.72
  164.6 2.4 fusion.2
  167.1 1.4 exponential_reduce_fusion
  168.6 1.2 copy-done.1
  169.8 3.7 fusion.66
  173.5 12.7 %fusion.27 = f32[2,512,3,64]{1,3,2,0:T(8,128)S(1)} fusion(f32[2,3,512,512]{2,3,1,0:T(8,128)} %fusion.66, bf16[2,512,3,48]{1,3,2,0:T(8,128)(2,1)S(1)} %copy-done.21, bf16[2,512,3,16]{1,3,2,0:T(8,128)(2,1)S(1)} %copy-done.28, f32[2,3,512,512]{2,3,1,0:T(8,128)} %copy-done.1, f32[2,3,512]{2,1,0:T(4,128)S(1)} %log_add_fusion, pred[2,512,512]{1,2,0:T(8,128)(4,1)S(1)} %copy-done.8), kind=kOutput, calls=%fused_computation.31 | convolution fusion | flops 219418112 | bytes 14299136 | tf_op jit(solution)/shard_map/bhqk,bkhd->bqhd/dot_general | solution.py:89
  187.1 12.8 %fusion.30 = f32[2,512,3,64]{1,3,2,0:T(8,128)S(1)} fusion(f32[2,3,512,512]{2,3,1,0:T(8,128)} %fusion.66, bf16[2,512,3,48]{1,3,2,0:T(8,128)(2,1)S(1)} %copy-done.23, bf16[2,512,3,16]{1,3,2,0:T(8,128)(2,1)S(1)} %copy-done.26, f32[2,3,512,512]{2,3,1,0:T(8,128)} %copy-done.1, f32[2,3,512]{2,1,0:T(4,128)S(1)} %log_add_fusion, pred[2,512,512]{1,2,0:T(8,128)(4,1)S(1)} %copy-done.8), kind=kOutput, calls=%fused_computation.32 | convolution fusion | flops 219418112 | bytes 14299136 | tf_op jit(solution)/shard_map/bhqk,bqhd->bkhd/dot_general | solution.py:92
  200.0 0.9 slice.101
  200.9 4.5 fusion.36
  205.9 1.1 slice_multiply_fusion.3
  207.1 5.5 multiply_convert_fusion.1
  212.6 5.6 fusion.90
  218.1 1.3 reshape.185
  219.4 1.5 copy.103
  221.0 1.7 maximum_add_fusion
  222.7 1.1 maximum_bitcast_fusion
  223.8 1.6 convolution_bitcast_fusion
  225.4 1.2 maximum_bitcast_fusion.1
  226.6 4.8 fusion.24
  231.7 1.2 copy.93
  233.2 1.0 copy-done.12
  234.3 3.2 fusion.92
  237.6 4.8 fusion.62
  242.7 3.2 fusion.91
  245.9 2.3 convolution_add_fusion
  248.3 4.5 fusion.93
  252.9 4.7 fusion.60
  257.6 4.3 fusion.94
  262.0 1.3 dynamic-slice.4
  264.0 0.9 dynamic-update-slice.4
  265.6 1.3 fusion.18
  267.1 12.8 %all-reduce.10 = f32[3,192]{1,0:T(4,128)S(1)} all-reduce(f32[3,192]{1,0:T(4,128)S(1)} %reshape.184), channel_id=10, replica_groups=mesh['dp'=8,'tensor'=4] {'dp'}, use_global_device_ids=true, to_apply=%region_20.21.clone | all-reduce | flops 576 | bytes 4608
  280.5 1.4 copy.104
  281.9 10.3 %reduce-scatter.26.cloned.1.call-done = f32[96,192]{1,0:T(8,128)} async-done(((f32[768,192]{1,0:T(8,128)}), f32[96,192]{1,0:T(8,128)}) %reduce-scatter.26.cloned.1.call-update) | async-done | bytes 73744
  292.2 1.6 copy.102
  293.8 61.1 %reduce-scatter.16.cloned.1.call-done = f32[256,768]{1,0:T(8,128)} async-done(((f32[1024,768]{1,0:T(8,128)}), f32[256,768]{1,0:T(8,128)}) %reduce-scatter.16.cloned.1.call-update) | async-done | bytes 786448 | tf_op jit(solution)/shard_map/reduce_scatter | solution.py:218
  354.9 62.6 %reduce-scatter.18.cloned.1.call-done = f32[256,768]{1,0:T(8,128)} async-done(((f32[1024,768]{1,0:T(8,128)}), f32[256,768]{1,0:T(8,128)}) %reduce-scatter.18.cloned.1.call-update) | async-done | bytes 786448 | tf_op jit(solution)/shard_map/reduce_scatter | solution.py:219
  417.6 1.9 fusion.86
  419.5 1.2 fusion.54
  420.7 43.6 %all-reduce.12 = (f32[768]{0:T(1024)S(1)}, f32[768]{0:T(1024)S(1)}, f32[768]{0:T(1024)S(1)}, f32[768]{0:T(1024)S(1)}, f32[768]{0:T(1024)S(1)}, /*index=5*/f32[768]{0:T(1024)S(1)}, f32[768]{0:T(1024)S(1)}) all-reduce(f32[768]{0:T(1024)S(1)} %dynamic-update-slice.5, ...), channel_id=1, replica_groups=mesh['dp'=8,'tensor'=4] {'dp','tensor'}, use_global_device_ids=true, to_apply=%add.5 | all-reduce | flops 5376 | bytes 43008
  466.7 14.4 %reduce-scatter.14.cloned.1.call-done = f32[256,768]{1,0:T(8,128)} async-done(((f32[1024,768]{1,0:T(8,128)}), f32[256,768]{1,0:T(8,128)}) %reduce-scatter.14.cloned.1.call-update) | async-done | bytes 786448 | tf_op jit(solution)/shard_map/reduce_scatter | solution.py:179
  481.1 2.1 fusion.59
  483.2 41.9 %reduce-scatter.20.cloned.1.call-done = f32[96,576]{1,0:T(8,128)} async-done(((f32[768,576]{1,0:T(8,128)}), f32[96,576]{1,0:T(8,128)}) %reduce-scatter.20.cloned.1.call-update) | async-done | bytes 221200 | tf_op jit(solution)/shard_map/reduce_scatter | solution.py:244
  525.1 46.3 %reduce-scatter.22.cloned.1.call-done = f32[96,768]{1,0:T(8,128)} async-done(((f32[768,768]{1,0:T(8,128)}), f32[96,768]{1,0:T(8,128)}) %reduce-scatter.22.cloned.1.call-update) | async-done | bytes 294928 | tf_op jit(solution)/shard_map/reduce_scatter | solution.py:245
  571.4 46.2 %reduce-scatter.24.cloned.1.call-done = f32[768,96]{0,1:T(8,128)} async-done(((f32[768,768]{0,1:T(8,128)}), f32[768,96]{0,1:T(8,128)}) %reduce-scatter.24.cloned.1.call-update) | async-done | bytes 294928 | tf_op jit(solution)/shard_map/reduce_scatter | solution.py:249
  (146 shorter events, 17.0 us)
Async XLA Ops:
  7.2 116.5 %all-gather.7.cloned.1.call-start = ((), (), s32[]{:S(2)}) async-start(), calls=%async_computation.9 | async-start | bytes 1966080 | tf_op jit(solution)/shard_map/all_gather | solution.py:157
  57.2 103.8 %all-gather.13.cloned.1.call-start = ((), (), s32[]{:S(2)}) async-start(), calls=%async_computation.13 | async-start | bytes 1966080 | tf_op jit(solution)/shard_map/all_gather | solution.py:189
  59.2 7.3 %copy-start.24 = (bf16[96,576]{1,0:T(8,128)(2,1)S(1)}, bf16[96,576]{1,0:T(8,128)(2,1)}, u32[]{:S(2)}) copy-start(bf16[96,576]{1,0:T(8,128)(2,1)} %param.22) | copy-start | bytes 331780
  59.3 147.8 %all-gather.9.cloned.1.call-start = ((), (), s32[]{:S(2)}) async-start(), calls=%async_computation.10 | async-start | bytes 1327104 | tf_op jit(solution)/shard_map/all_gather | solution.py:140
  60.0 18.1 %copy-start.32 = (bf16[3,24]{1,0:T(4,128)(2,1)S(1)}, bf16[3,24]{1,0:T(4,128)(2,1)}, u32[]{:S(2)}) copy-start(bf16[3,24]{1,0:T(4,128)(2,1)} %param.23) | copy-start | bytes 436
  60.0 27.1 %copy-start.29 = (bf16[192,96]{1,0:T(8,128)(2,1)S(1)}, bf16[192,96]{1,0:T(8,128)(2,1)}, u32[]{:S(2)}) copy-start(bf16[192,96]{1,0:T(8,128)(2,1)} %param.24) | copy-start | bytes 110596
  61.3 35.4 %copy-start.33 = (bf16[3,32]{1,0:T(4,128)(2,1)S(1)}, bf16[3,32]{1,0:T(4,128)(2,1)}, u32[]{:S(2)}) copy-start(bf16[3,32]{1,0:T(4,128)(2,1)} %param.27) | copy-start | bytes 580
  61.3 44.2 %copy-start.30 = (s32[2,512]{1,0:T(2,128)S(1)}, s32[2,512]{1,0:T(2,128)}, u32[]{:S(2)}) copy-start(s32[2,512]{1,0:T(2,128)} %param.16) | copy-start | bytes 12292
  61.3 145.8 %all-to-all-start = ((bf16[4,256,768]{2,1,0:T(8,128)(2,1)}), bf16[4,256,768]{2,1,0:T(8,128)(2,1)}, u32[]{:S(2)}, u32[]{:S(2)}) async-start(bf16[4,256,768]{2,1,0:T(8,128)(2,1)} %stack.19), calls=%async_computation | async-start | bytes 3145728 | tf_op jit(solution)/shard_map/all_to_all | solution.py:159
  65.8 146.8 %all-gather.11.cloned.1.call-start = ((), (), s32[]{:S(2)}) async-start(), calls=%async_computation.11 | async-start | bytes 1327104 | tf_op jit(solution)/shard_map/all_gather | solution.py:144
  66.3 214.2 %reduce-scatter.28.cloned.1.call-start = ((), (), s32[]{:S(2)}) async-start(), calls=%async_computation.20 | async-start | bytes 147456
  78.1 45.6 %copy-start.13 = (bf16[768,576]{1,0:T(8,128)(2,1)}, bf16[768,576]{1,0:T(8,128)(2,1)S(1)}, u32[]{:S(2)}) copy-start(bf16[768,576]{1,0:T(8,128)(2,1)S(1)} %all_gather.49) | copy-start | bytes 2654212
  132.4 2.2 copy-start.7
  136.3 27.1 %copy-start.15 = (f32[2,512,3,8]{1,3,2,0:T(8,128)S(1)}, f32[2,512,3,8]{1,3,2,0:T(8,128)}, u32[]{:S(2)}) copy-start(f32[2,512,3,8]{1,3,2,0:T(8,128)} %get-tuple-element.42) | copy-start | bytes 294916
  136.3 27.1 %copy-start.16 = (f32[2,512,3,8]{1,3,2,0:T(8,128)S(1)}, f32[2,512,3,8]{1,3,2,0:T(8,128)}, u32[]{:S(2)}) copy-start(f32[2,512,3,8]{1,3,2,0:T(8,128)} %get-tuple-element.43) | copy-start | bytes 294916
  136.3 27.1 %copy-start.17 = (f32[2,512,3,8]{1,3,2,0:T(8,128)S(1)}, f32[2,512,3,8]{1,3,2,0:T(8,128)}, u32[]{:S(2)}) copy-start(f32[2,512,3,8]{1,3,2,0:T(8,128)} %get-tuple-element.40) | copy-start | bytes 294916
  136.3 27.1 %copy-start.18 = (f32[2,512,3,8]{1,3,2,0:T(8,128)S(1)}, f32[2,512,3,8]{1,3,2,0:T(8,128)}, u32[]{:S(2)}) copy-start(f32[2,512,3,8]{1,3,2,0:T(8,128)} %get-tuple-element.41) | copy-start | bytes 294916
  136.3 28.3 %copy-start.20 = (bf16[2,512,3,48]{1,3,2,0:T(8,128)(2,1)S(1)}, bf16[2,512,3,48]{1,3,2,0:T(8,128)(2,1)}, u32[]{:S(2)}) copy-start(bf16[2,512,3,48]{1,3,2,0:T(8,128)(2,1)} %slice.122) | copy-start | bytes 884740
  136.4 28.3 %copy-start.22 = (bf16[2,512,3,48]{1,3,2,0:T(8,128)(2,1)S(1)}, bf16[2,512,3,48]{1,3,2,0:T(8,128)(2,1)}, u32[]{:S(2)}) copy-start(bf16[2,512,3,48]{1,3,2,0:T(8,128)(2,1)} %slice.123) | copy-start | bytes 884740
  163.4 6.4 %copy-start.9 = (bf16[2,512,3,64]{1,0,3,2:T(2,128)(2,1)}, bf16[2,512,3,64]{1,0,3,2:T(2,128)(2,1)S(1)}, u32[]{:S(2)}) copy-start(bf16[2,512,3,64]{1,0,3,2:T(2,128)(2,1)S(1)} %reshape.183) | copy-start | bytes 1179652
  164.6 2.5 copy-start.25
  164.6 2.5 copy-start.27
  164.6 2.5 copy-start.8
  167.1 2.6 copy-start.1
  167.1 2.7 copy-start.10
  169.8 31.1 %copy-start.31 = (f32[2,3,512]{2,1,0:T(4,128)}, f32[2,3,512]{2,1,0:T(4,128)S(1)}, u32[]{:S(2)}) copy-start(f32[2,3,512]{2,1,0:T(4,128)S(1)} %log_add_fusion) | copy-start | bytes 36868
  169.8 3.7 copy-start.21
  169.8 3.7 copy-start.28
  173.5 13.5 %copy-start.23 = (bf16[2,512,3,48]{1,3,2,0:T(8,128)(2,1)S(1)}, bf16[2,512,3,48]{1,3,2,0:T(8,128)(2,1)}, u32[]{:S(2)}) copy-start(bf16[2,512,3,48]{1,3,2,0:T(8,128)(2,1)} %slice.123) | copy-start | bytes 884740
  173.5 13.5 %copy-start.26 = (bf16[2,512,3,16]{1,3,2,0:T(8,128)(2,1)S(1)}, bf16[2,512,3,16]{1,3,2,0:T(8,128)(2,1)}, u32[]{:S(2)}) copy-start(bf16[2,512,3,16]{1,3,2,0:T(8,128)(2,1)} %copy-done.25) | copy-start | bytes 294916
  199.9 5.5 copy-start.11
  200.9 5.0 copy-start.19
  205.9 17.9 %copy-start.3 = (bf16[24,8,2,512]{3,1,2,0:T(8,128)(2,1)}, bf16[24,8,2,512]{3,1,2,0:T(8,128)(2,1)S(1)}, u32[]{:S(2)}) copy-start(bf16[24,8,2,512]{3,1,2,0:T(8,128)(2,1)S(1)} %copy.108) | copy-start | bytes 1179652
  207.1 5.5 copy-start.2
  220.9 71.3 %reduce-scatter.26.cloned.1.call-start = ((), (), s32[]{:S(2)}) async-start(), calls=%async_computation.19 | async-start | bytes 884736
  226.6 128.3 %reduce-scatter.16.cloned.1.call-start = ((), (), s32[]{:S(2)}) async-start(), calls=%async_computation.14 | async-start | bytes 3932160 | tf_op jit(solution)/shard_map/reduce_scatter | solution.py:218
  231.4 1.8 copy-start.5
  231.7 2.6 copy-start.14
  233.2 1.0 copy-start.12
  237.5 180.0 %reduce-scatter.18.cloned.1.call-start = ((), (), s32[]{:S(2)}) async-start(), calls=%async_computation.15 | async-start | bytes 3932160 | tf_op jit(solution)/shard_map/reduce_scatter | solution.py:219
  242.4 238.7 %reduce-scatter.14.cloned.1.call-start = ((), (), s32[]{:S(2)}) async-start(), calls=%async_computation.12 | async-start | bytes 3932160 | tf_op jit(solution)/shard_map/reduce_scatter | solution.py:179
  242.7 3.2 copy-start.4
  248.2 276.9 %reduce-scatter.20.cloned.1.call-start = ((), (), s32[]{:S(2)}) async-start(), calls=%async_computation.16 | async-start | bytes 2211840 | tf_op jit(solution)/shard_map/reduce_scatter | solution.py:244
  252.8 318.6 %reduce-scatter.22.cloned.1.call-start = ((), (), s32[]{:S(2)}) async-start(), calls=%async_computation.17 | async-start | bytes 2654208 | tf_op jit(solution)/shard_map/reduce_scatter | solution.py:245
  257.6 360.0 %reduce-scatter.24.cloned.1.call-start = ((), (), s32[]{:S(2)}) async-start(), calls=%async_computation.18 | async-start | bytes 2654208 | tf_op jit(solution)/shard_map/reduce_scatter | solution.py:249
  261.9 155.6 %copy-start = (bf16[256,768]{1,0:T(8,128)(2,1)S(1)}, bf16[256,768]{1,0:T(8,128)(2,1)}, u32[]{:S(2)}) copy-start(bf16[256,768]{1,0:T(8,128)(2,1)} %param.15) | copy-start | bytes 1179652
  261.9 157.5 %copy-start.6 = (f32[256,768]{1,0:T(8,128)S(1)}, f32[256,768]{1,0:T(8,128)}, u32[]{:S(2)}) copy-start(f32[256,768]{1,0:T(8,128)} %param.17) | copy-start | bytes 2359300
  464.4 153.7 %copy-start.34 = (f32[24]{0:T(128)}, f32[24]{0:T(128)S(1)}, u32[]{:S(2)}) copy-start(f32[24]{0:T(128)S(1)} %dynamic-slice.6) | copy-start | bytes 292
Sparse Core Ops, SparseCore 0:
  57.4 66.2 all-gather.6
  125.2 35.7 all-gather.12
  162.9 22.7 all-gather.8
  187.5 23.9 all-gather.10
  221.0 32.4 reduce-scatter.27
  257.1 35.0 reduce-scatter.25
  294.5 60.3 reduce-scatter.15
  357.2 60.3 reduce-scatter.17
  419.9 61.2 reduce-scatter.13
  485.0 40.1 reduce-scatter.19
  529.1 42.3 reduce-scatter.21
  575.2 42.3 reduce-scatter.23
